TPU v7x, 128 devices: a whole 4x4x4 slice. The times are simulated.
128 devices in a mesh: dp: 16 (over y_hi, z, core), tensor: 8 (over x, y_lo).
Axes of the slice: x: 4, y: 4 (y_hi: 2, y_lo: 2; y = y_hi * 2 + y_lo), z: 4, core: 2. Of those that a mesh axis runs over, the one named last changes fastest.
Arguments:
- activations: bfloat16 [16384, 8192], P('dp'), may hold values from -6 to 6
- out_grad: bfloat16 [16384, 28672], P('dp', 'tensor'), may hold values from -0.046875 to 0.046875
- projector: bfloat16 [8192, 512], P(('dp', 'tensor')), may hold values from -0.0625 to 0.0625
- first_moment: float32 [512, 28672], P('dp', 'tensor'), may hold values from -3 to 3
- second_moment: float32 [512, 28672], P('dp', 'tensor'), may hold values from 0.1 to 4
Outputs:
- update: float32 [8192, 28672], P('dp', 'tensor')
- new_first: float32 [512, 28672], P('dp', 'tensor')
- new_second: float32 [512, 28672], P('dp', 'tensor')
All inputs are finite; a program needn't handle non-finite values.
Results may differ from a plain program's by a relative error of at most 0.0031.
Values may be sent and summed in bfloat16 or wider, within the bound.
A program may use at most 128 MiB of HBM per device.

v0:
```python
import jax
import jax.numpy as jnp
from jax import lax
from jax.sharding import PartitionSpec as P

beta_one = 0.9
beta_two = 0.999
bias_one = 1.0 - 0.9**10
bias_two = 1.0 - 0.999**10
adam_eps = 1e-08


def in_order(tiles, dim):
    dims = list(tiles.shape[1:])
    dims[dim] *= tiles.shape[0]
    return jnp.moveaxis(tiles, 0, dim).reshape(dims)


def sent_to_all(shard, axis):
    copies = jnp.broadcast_to(shard, (lax.axis_size(axis), *shard.shape))
    return lax.all_to_all(copies, axis, split_axis=0, concat_axis=0, tiled=True)


def collect(shard, axis, dim):
    return in_order(sent_to_all(shard, axis), dim)


def per_device(activations, out_grad, projector, first_moment, second_moment):
    token_rows = activations.shape[0]
    lane_blocks = collect(projector, "dp", 0)
    data_lanes = lax.axis_size("dp")
    tensor_lanes = lax.axis_size("tensor")
    block_rows = projector.shape[0]
    split_cols = activations.reshape(token_rows, data_lanes, tensor_lanes, block_rows)
    chosen = lax.dynamic_index_in_dim(split_cols, lax.axis_index("tensor"), 2, keepdims=False)
    chosen = chosen.reshape(token_rows, data_lanes * block_rows)
    partial_sum = jnp.dot(chosen, lane_blocks, preferred_element_type=jnp.float32)
    projected = lax.psum(partial_sum, "tensor")
    projected = projected.astype(jnp.bfloat16)
    coefficients = lax.psum_scatter(
        lax.dot_general(
            projected, out_grad, (((0,), (0,)), ((), ())), preferred_element_type=jnp.float32
        ),
        "dp",
        scatter_dimension=0,
        tiled=True,
    )
    new_first = beta_one * first_moment + (1.0 - beta_one) * coefficients
    new_second = beta_two * second_moment + (1.0 - beta_two) * coefficients * coefficients
    normalized = (new_first / bias_one / (jnp.sqrt(new_second / bias_two) + adam_eps)).astype(
        jnp.bfloat16
    )
    basis_rows = collect(projector, "tensor", 0)
    update = jnp.dot(
        basis_rows,
        lax.all_gather(normalized, "dp", axis=0, tiled=True),
        preferred_element_type=jnp.float32,
    )
    return (update, new_first, new_second)


def solution(mesh):
    in_specs = (
        P("dp", None),
        P("dp", "tensor"),
        P(("dp", "tensor"), None),
        P("dp", "tensor"),
        P("dp", "tensor"),
    )
    out_specs = (P("dp", "tensor"), P("dp", "tensor"), P("dp", "tensor"))
    return jax.shard_map(
        per_device, mesh=mesh, in_specs=in_specs, out_specs=out_specs, check_vma=False
    )
```

profile of v0, /device:TPU:1, one launch (start us, length us, event | category | flops | bytes accessed | tf_op | source)
XLA Modules:
  0.0 319.9 jit_solution(16738832030383836894)
XLA Ops:
  7.2 1.9 broadcast_in_dim.6
  9.1 9.4 %all-to-all-start = ((bf16[16,64,512]{2,1,0:T(8,128)(2,1)}), bf16[16,64,512]{2,1,0:T(8,128)(2,1)S(1)}, u32[]{:S(2)}, u32[]{:S(2)}) async-start(bf16[16,64,512]{2,1,0:T(8,128)(2,1)} %broadcast_in_dim.6), calls=%async_computation | async-start | bytes 2097152 | tf_op jit(solution)/shard_map/all_to_all | solution.py:21
  18.5 0.0 reduce-scatter.2.cloned.1.call-start
  18.6 22.4 %copy.9 = bf16[1024,8192]{0,1:T(8,128)(2,1)} copy(bf16[1024,8192]{1,0:T(8,128)(2,1)} %param.5) | data formatting | bytes 33554432 | tf_op args[0]
  41.0 3.1 constant_dynamic-slice_fusion
  44.2 0.0 all-to-all-done
  44.2 2.9 fusion.4
  47.0 84.2 %all-reduce.1 = bf16[1024,512]{1,0:T(8,128)(2,1)S(1)} all-reduce(f32[1024,512]{1,0:T(8,128)S(1)} %fusion.4), channel_id=1, replica_groups=mesh['dp'=16,'tensor'=8] {'tensor'}, use_global_device_ids=true, to_apply=%region_0.1 | all-reduce | flops 524288 | bytes 3145728 | tf_op jit(solution)/shard_map/psum | solution.py:38
  131.3 9.2 %fusion.5 = f32[512,3584]{1,0:T(8,128)} fusion(bf16[1024,512]{1,0:T(8,128)(2,1)S(1)} %all-reduce.1, bf16[1024,3584]{1,0:T(8,128)(2,1)} %param.6), kind=kOutput, calls=%fused_computation.9 | convolution fusion | flops 3758096384 | bytes 15728640 | tf_op jit(solution)/shard_map/dot_general | solution.py:41
  140.4 0.0 copy-start
  140.4 0.0 copy-start.1
  140.4 0.0 copy-start.2
  140.4 0.0 reduce-scatter.2.cloned.1.call-update
  140.5 0.0 all-gather.2.cloned.1.call-start
  140.5 100.7 %reduce-scatter.2.cloned.1.call-done = f32[32,3584]{1,0:T(8,128)} async-done(((f32[512,3584]{1,0:T(8,128)}), f32[32,3584]{1,0:T(8,128)}) %reduce-scatter.2.cloned.1.call-update) | async-done | bytes 458768 | tf_op jit(solution)/shard_map/reduce_scatter | solution.py:40
  241.2 0.0 copy-done
  241.2 0.0 copy-done.1
  241.2 2.2 divide_convert_fusion
  243.4 0.0 all-gather.2.cloned.1.call-update
  243.4 0.0 copy-done.2
  243.5 11.2 %all_to_all.10 = bf16[8,64,512]{2,1,0:T(8,128)(2,1)S(1)} all-to-all(bf16[8,64,512]{2,1,0:T(8,128)(2,1)S(1)} %broadcast_in_dim.7), channel_id=1, replica_groups=mesh['dp'=16,'tensor'=8] {'tensor'}, dimensions={0} | all-to-all | bytes 1048576 | tf_op jit(solution)/shard_map/all_to_all | solution.py:21
  254.7 42.9 %all-gather.2.cloned.1.call-done = bf16[512,3584]{1,0:T(8,128)(2,1)} async-done(((bf16[32,3584]{1,0:T(8,128)(2,1)}), bf16[512,3584]{1,0:T(8,128)(2,1)}) %all-gather.2.cloned.1.call-update) | async-done | bytes 3670032 | tf_op jit(solution)/shard_map/all_gather | solution.py:56
  297.6 7.1 %convolution_bitcast_fusion = f32[512,3584]{0,1:T(8,128)} fusion(bf16[512,3584]{1,0:T(8,128)(2,1)} %all-gather.2.cloned.1.call-done, bf16[512,512]{1,0:T(8,128)(2,1)S(1)} %bitcast.13), kind=kOutput, calls=%fused_computation | convolution fusion | flops 1879048192 | bytes 11534336 | tf_op jit(solution)/shard_map/dot_general | solution.py:54
  304.7 8.4 %copy.10 = f32[512,3584]{1,0:T(8,128)} copy(f32[512,3584]{0,1:T(8,128)} %convolution_bitcast_fusion) | data formatting | bytes 14680064
  (1 shorter events, 0.0 us)
Async XLA Ops:
  9.1 35.1 %all-to-all-start = ((bf16[16,64,512]{2,1,0:T(8,128)(2,1)}), bf16[16,64,512]{2,1,0:T(8,128)(2,1)S(1)}, u32[]{:S(2)}, u32[]{:S(2)}) async-start(bf16[16,64,512]{2,1,0:T(8,128)(2,1)} %broadcast_in_dim.6), calls=%async_computation | async-start | bytes 2097152 | tf_op jit(solution)/shard_map/all_to_all | solution.py:21
  18.5 222.7 %reduce-scatter.2.cloned.1.call-start = ((), (), s32[]{:S(2)}) async-start(), calls=%async_computation.3 | async-start | bytes 7798784 | tf_op jit(solution)/shard_map/reduce_scatter | solution.py:40
  140.4 100.8 %copy-start = (f32[32,3584]{1,0:T(8,128)S(1)}, f32[32,3584]{1,0:T(8,128)}, u32[]{:S(2)}) copy-start(f32[32,3584]{1,0:T(8,128)} %param.8) | copy-start | bytes 1376260
  140.4 100.8 %copy-start.1 = (f32[32,3584]{1,0:T(8,128)S(1)}, f32[32,3584]{1,0:T(8,128)}, u32[]{:S(2)}) copy-start(f32[32,3584]{1,0:T(8,128)} %param.9) | copy-start | bytes 1376260
  140.4 103.0 %copy-start.2 = (bf16[64,512]{1,0:T(8,128)(2,1)S(1)}, bf16[64,512]{1,0:T(8,128)(2,1)}, u32[]{:S(2)}) copy-start(bf16[64,512]{1,0:T(8,128)(2,1)} %param.7) | copy-start | bytes 196612
  140.5 157.1 %all-gather.2.cloned.1.call-start = ((), (), s32[]{:S(2)}) async-start(), calls=%async_computation.4 | async-start | bytes 3899392 | tf_op jit(solution)/shard_map/all_gather | solution.py:56
Sparse Core Ops, SparseCore 0:
  140.6 100.6 reduce-scatter.1
  244.3 53.2 all-gather.1
where the time goes:
time: 321 us; the launch traced here: 320 us
  waiting for transfers between devices  144 us (45%)
  blocking collectives  95.4 us (30%)
  local copies, waits for them, and re-layouts  35.9 us (11%)
  matrix products  19.1 us (6%)
  between operations  14.1 us (4%)
  starting transfers between devices  9.53 us (3%)
    reduce_scatter x1, waiting for transfers between devices, per_device(): lax.psum_scatter(lax.dot_general(projected, out_grad, (((0,), (0,)), ((),...  101 us
    psum x1, blocking collectives, per_device(): projected = lax.psum(partial_sum, 'tensor')  84.2 us
    all_gather x1, waiting for transfers between devices, per_device(): lax.all_gather(normalized, 'dp', axis=0, tiled=True)  42.9 us
    unnamed x8, local copies, waits for them, and re-layouts  30.8 us
    all_to_all x1, blocking collectives, sent_to_all(): return lax.all_to_all(copies, axis, split_axis=0, concat_axis=0, tiled=True)  11.2 us
    all_to_all x1, starting transfers between devices, sent_to_all(): return lax.all_to_all(copies, axis, split_axis=0, concat_axis=0, tiled=True)  9.45 us
    dot_general x1, matrix products, per_device(): lax.dot_general(projected, out_grad, (((0,), (0,)), ((), ())), preferred_...  9.15 us
    dot_general x1, matrix products, per_device(): jnp.dot(basis_rows, lax.all_gather(normalized, 'dp', axis=0, tiled=True),...  7.12 us
  transfers between devices with their start and end apart: 3, of which 2 were waited for; matrix products, arithmetic and copies ran while one was open for 8% of the time, Pallas kernels for 0%

commit v1 on v0

--- a/solution.py
+++ b/solution.py
@@ -8,6 +8,12 @@
 bias_one = 1.0 - 0.9**10
 bias_two = 1.0 - 0.999**10
 adam_eps = 1e-08
+
+
+def add_all(x, axis):
+    pieces = lax.all_gather(x, axis, axis=0, tiled=False)
+    total = pieces.sum(axis=0)
+    return total
 
 
 def in_order(tiles, dim):
@@ -35,7 +41,7 @@
     chosen = lax.dynamic_index_in_dim(split_cols, lax.axis_index("tensor"), 2, keepdims=False)
     chosen = chosen.reshape(token_rows, data_lanes * block_rows)
     partial_sum = jnp.dot(chosen, lane_blocks, preferred_element_type=jnp.float32)
-    projected = lax.psum(partial_sum, "tensor")
+    projected = add_all(partial_sum, "tensor")
     projected = projected.astype(jnp.bfloat16)
     coefficients = lax.psum_scatter(
         lax.dot_general(

time: 321 us -> 563 us (1.75)
  waiting for transfers between devices: 144 us -> 464 us
  blocking collectives: 95.4 us -> 11 us
  other arithmetic: 2.16 us -> 10.3 us
    all_gather x0 -> x1, waiting for transfers between devices: none -> 327 us  [add_all(): pieces = lax.all_gather(x, axis, axis=0, tiled=False)]
    psum x1 -> x0, blocking collectives: 84.2 us -> none  [per_device(): projected = lax.psum(partial_sum, 'tensor')]
    reduce_sum x0 -> x1, other arithmetic: none -> 8.09 us  [add_all(): total = pieces.sum(axis=0)]
    reduce_scatter x1, waiting for transfers between devices: 101 us -> 94.4 us  [per_device(): lax.psum_scatter(lax.dot_general(projected, out_grad, (((0,), (0,)), ((),...]
  transfers between devices with their start and end apart: 3 -> 4, of which waited for: 2 -> 3; matrix products, arithmetic and copies ran while one was open for 8% -> 4% of each run, Pallas kernels for 0% -> 0%
where the time goes in v1:
time: 563 us; the launch traced here: 562 us
  waiting for transfers between devices  464 us (82%)
  local copies, waits for them, and re-layouts  34.6 us (6%)
  matrix products  18.9 us (3%)
  between operations  13.8 us (2%)
  blocking collectives  11 us (2%)
  other arithmetic  10.3 us (2%)
  starting transfers between devices  9.57 us (2%)
    all_gather x1, waiting for transfers between devices, add_all(): pieces = lax.all_gather(x, axis, axis=0, tiled=False)  327 us
    reduce_scatter x1, waiting for transfers between devices, per_device(): lax.psum_scatter(lax.dot_general(projected, out_grad, (((0,), (0,)), ((),...  94.4 us
    all_gather x1, waiting for transfers between devices, per_device(): lax.all_gather(normalized, 'dp', axis=0, tiled=True)  43 us
    unnamed x8, local copies, waits for them, and re-layouts  30.8 us
  transfers between devices with their start and end apart: 4, of which 3 were waited for; matrix products, arithmetic and copies ran while one was open for 4% of the time, Pallas kernels for 0%

profile of v1, /device:TPU:1, one launch (start us, length us, event | category | flops | bytes accessed | tf_op | source)
XLA Modules:
  0.0 562.0 jit_solution(8712035614415802570)
XLA Ops:
  7.2 1.9 broadcast_in_dim.6
  9.1 9.4 %all-to-all-start = ((bf16[16,64,512]{2,1,0:T(8,128)(2,1)}), bf16[16,64,512]{2,1,0:T(8,128)(2,1)S(1)}, u32[]{:S(2)}, u32[]{:S(2)}) async-start(bf16[16,64,512]{2,1,0:T(8,128)(2,1)} %broadcast_in_dim.6), calls=%async_computation | async-start | bytes 2097152 | tf_op jit(solution)/shard_map/all_to_all | solution.py:27
  18.5 0.0 all-gather.6.cloned.1.call-start
  18.6 22.4 %copy.9 = bf16[1024,8192]{0,1:T(8,128)(2,1)} copy(bf16[1024,8192]{1,0:T(8,128)(2,1)} %param.5) | data formatting | bytes 33554432 | tf_op args[0]
  41.0 1.9 constant_dynamic-slice_fusion
  42.8 0.0 all-to-all-done
  42.8 2.6 fusion.4
  45.4 0.0 all-gather.6.cloned.1.call-update
  45.5 0.0 reduce-scatter.2.cloned.1.call-start
  45.5 326.5 %all-gather.6.cloned.1.call-done = f32[8192,512]{1,0:T(8,128)} async-done(((f32[1024,512]{1,0:T(8,128)}), f32[8192,512]{1,0:T(8,128)}) %all-gather.6.cloned.1.call-update) | async-done | bytes 16777232 | tf_op jit(solution)/shard_map/all_gather | solution.py:14
  372.0 8.1 %reduce_sum.9 = bf16[1024,512]{1,0:T(8,128)(2,1)S(1)} reduce(f32[8,1024,512]{2,1,0:T(8,128)} %bitcast.14, f32[]{:T(128)} %constant.8.clone.1), dimensions={0}, to_apply=%region_0.1 | reduce | flops 3670016 | bytes 17825796 | tf_op jit(solution)/shard_map/reduce_sum | solution.py:15
  380.1 9.2 %fusion.5 = f32[512,3584]{1,0:T(8,128)} fusion(bf16[1024,512]{1,0:T(8,128)(2,1)S(1)} %reduce_sum.9, bf16[1024,3584]{1,0:T(8,128)(2,1)} %param.6), kind=kOutput, calls=%fused_computation.9 | convolution fusion | flops 3758096384 | bytes 15728640 | tf_op jit(solution)/shard_map/dot_general | solution.py:47
  389.3 0.0 copy-start
  389.3 0.0 copy-start.1
  389.3 0.0 copy-start.2
  389.3 0.0 reduce-scatter.2.cloned.1.call-update
  389.3 0.0 all-gather.4.cloned.1.call-start
  389.4 94.4 %reduce-scatter.2.cloned.1.call-done = f32[32,3584]{1,0:T(8,128)} async-done(((f32[512,3584]{1,0:T(8,128)}), f32[32,3584]{1,0:T(8,128)}) %reduce-scatter.2.cloned.1.call-update) | async-done | bytes 458768 | tf_op jit(solution)/shard_map/reduce_scatter | solution.py:46
  483.8 0.0 copy-done
  483.8 0.0 copy-done.1
  483.8 2.2 divide_convert_fusion
  485.9 0.0 all-gather.4.cloned.1.call-update
  485.9 0.0 copy-done.2
  486.0 11.0 %all_to_all.10 = bf16[8,64,512]{2,1,0:T(8,128)(2,1)S(1)} all-to-all(bf16[8,64,512]{2,1,0:T(8,128)(2,1)S(1)} %broadcast_in_dim.7), channel_id=1, replica_groups=mesh['dp'=16,'tensor'=8] {'tensor'}, dimensions={0} | all-to-all | bytes 1048576 | tf_op jit(solution)/shard_map/all_to_all | solution.py:27
  497.0 43.0 %all-gather.4.cloned.1.call-done = bf16[512,3584]{1,0:T(8,128)(2,1)} async-done(((bf16[32,3584]{1,0:T(8,128)(2,1)}), bf16[512,3584]{1,0:T(8,128)(2,1)}) %all-gather.4.cloned.1.call-update) | async-done | bytes 3670032 | tf_op jit(solution)/shard_map/all_gather | solution.py:62
  540.0 7.1 %convolution_bitcast_fusion = f32[512,3584]{0,1:T(8,128)} fusion(bf16[512,3584]{1,0:T(8,128)(2,1)} %all-gather.4.cloned.1.call-done, bf16[512,512]{1,0:T(8,128)(2,1)S(1)} %bitcast.15), kind=kOutput, calls=%fused_computation | convolution fusion | flops 1879048192 | bytes 11534336 | tf_op jit(solution)/shard_map/dot_general | solution.py:60
  547.1 8.4 %copy.10 = f32[512,3584]{1,0:T(8,128)} copy(f32[512,3584]{0,1:T(8,128)} %convolution_bitcast_fusion) | data formatting | bytes 14680064
  (1 shorter events, 0.0 us)
Async XLA Ops:
  9.1 33.8 %all-to-all-start = ((bf16[16,64,512]{2,1,0:T(8,128)(2,1)}), bf16[16,64,512]{2,1,0:T(8,128)(2,1)S(1)}, u32[]{:S(2)}, u32[]{:S(2)}) async-start(bf16[16,64,512]{2,1,0:T(8,128)(2,1)} %broadcast_in_dim.6), calls=%async_computation | async-start | bytes 2097152 | tf_op jit(solution)/shard_map/all_to_all | solution.py:27
  18.5 353.5 %all-gather.6.cloned.1.call-start = ((), (), s32[]{:S(2)}) async-start(), calls=%async_computation.5 | async-start | bytes 18874368 | tf_op jit(solution)/shard_map/all_gather | solution.py:14
  45.5 438.3 %reduce-scatter.2.cloned.1.call-start = ((), (), s32[]{:S(2)}) async-start(), calls=%async_computation.3 | async-start | bytes 7798784 | tf_op jit(solution)/shard_map/reduce_scatter | solution.py:46
  389.3 94.5 %copy-start = (f32[32,3584]{1,0:T(8,128)S(1)}, f32[32,3584]{1,0:T(8,128)}, u32[]{:S(2)}) copy-start(f32[32,3584]{1,0:T(8,128)} %param.8) | copy-start | bytes 1376260
  389.3 94.5 %copy-start.1 = (f32[32,3584]{1,0:T(8,128)S(1)}, f32[32,3584]{1,0:T(8,128)}, u32[]{:S(2)}) copy-start(f32[32,3584]{1,0:T(8,128)} %param.9) | copy-start | bytes 1376260
  389.3 96.7 %copy-start.2 = (bf16[64,512]{1,0:T(8,128)(2,1)S(1)}, bf16[64,512]{1,0:T(8,128)(2,1)}, u32[]{:S(2)}) copy-start(bf16[64,512]{1,0:T(8,128)(2,1)} %param.7) | copy-start | bytes 196612
  389.3 150.7 %all-gather.4.cloned.1.call-start = ((), (), s32[]{:S(2)}) async-start(), calls=%async_computation.4 | async-start | bytes 3899392 | tf_op jit(solution)/shard_map/all_gather | solution.py:62
Sparse Core Ops, SparseCore 0:
  45.6 326.3 all-gather.5
  389.4 94.2 reduce-scatter.1
  486.8 53.1 all-gather.3
